TPU v7x, 32 devices: a whole 2x2x4 slice. The times are simulated.
32 devices in a mesh: row: 4 (over z), col: 2 (over x), pole: 4 (over y, core).
Axes of the slice: x: 2, y: 2, z: 4, core: 2. Of those that a mesh axis runs over, the one named last changes fastest.
Arguments:
- window: bfloat16 [4, 8192, 8192], P('pole', 'col', 'row'), may hold values from -6 to 6
- panels: bfloat16 [4, 2, 8192, 256], P('pole', 'col', 'row'), may hold values from -0.0625 to 0.0625
- row_map: int32 [3, 8192], P(None, 'row'), may hold values from 0 to 8191, as said below
- panel_root: int32 [4, 3], P('pole'), may hold values from 0 to 1
- upper_blocks: bfloat16 [4, 3, 256, 256], P('pole', None, 'row'), may hold values from -0.375 to 0.375
- diag_inverse: float32 [4, 3, 256, 256], P('pole', None, 'row'), may hold values from -6 to 6
- weights: float32 [4], replicated, may hold values from 0.25 to 1
- pole_order: int32 [4], P('pole'), may hold values from 0 to 3, each once
Outputs:
- inv_columns: float32 [3, 2, 4096, 256], P(None, 'col', ('row', 'pole'))
- inv_diag: float32 [3, 256, 256], P(None, ('row', 'pole'))
Inputs may be any that keep to these rules, and one draw needn't show every extreme that they name: row_map[k] permutes the positions inside each aligned group of 1024 consecutive positions. `pole_order`: each of the 4 poles appears once.
All inputs are finite; a program needn't handle non-finite values.
Results may differ from a plain program's by a relative error of at most 0.0003.
Values may be sent and summed in bfloat16 or wider, within the bound.
A program may use at most 128 MiB of HBM per device.

v0:
```python
import jax
import jax.numpy as jnp
from jax import lax
from jax.sharding import PartitionSpec as P

NS = 3


def precise(left, right):
    return jnp.dot(left, right, precision=lax.Precision.HIGHEST, preferred_element_type=jnp.float32)


def pair_index(current, earlier):
    return current * (current - 1) // 2 + earlier


def inverse_block(diagonals, crossed, first, second):
    if first == second:
        return diagonals[first]
    if first < second:
        return crossed[first, second]
    return crossed[second, first].T


def window_term(window_block, aligned):
    return jnp.dot(window_block, aligned, preferred_element_type=jnp.float32)


def shards(window, panels, row_map, panel_root, upper_blocks, diag_inverse, weights, pole_order):
    window_block = window[0]
    panel_slab = panels[0, 0]
    pole_roots = panel_root[0]
    band_rows = panel_slab.shape[0]
    group_rows = window_block.shape[0] // lax.axis_size("row")
    row_index = lax.axis_index("row")
    col_index = lax.axis_index("col")
    gathered_upper, gathered_inverse = (
        lax.all_gather(upper_blocks.astype(jnp.float32), "row", axis=2, tiled=True).astype(
            upper_blocks.dtype
        ),
        lax.all_gather(diag_inverse, "row", axis=2, tiled=True),
    )
    factors = gathered_upper[0].astype(jnp.float32)
    inverses = gathered_inverse[0]
    share_rows = inverses.shape[1] // lax.axis_size("row")
    slot_panels = lax.all_gather(panels, "col", axis=1, tiled=True)[0]
    pole_weight = jnp.sum(jnp.where(jnp.arange(weights.shape[0]) == pole_order[0], weights, 0.0))
    columns = []
    diagonals = []
    crossed = {}
    for current in range(NS):
        received = lax.dynamic_index_in_dim(slot_panels, pole_roots[current], 0, keepdims=False)
        aligned = jnp.take(received, row_map[current] - row_index * band_rows, axis=0)
        own_rows = lax.dynamic_slice_in_dim(aligned, col_index * group_rows, group_rows, 0).astype(
            jnp.float32
        )
        partials = [precise(columns[earlier].T, own_rows) for earlier in range(current)]
        window_sum = lax.psum_scatter(
            window_term(window_block, aligned), "row", scatter_dimension=0, tiled=True
        )
        y_window = window_sum
        for earlier in range(current):
            y_window = y_window + precise(columns[earlier], factors[pair_index(current, earlier)])
        congruence = precise(own_rows.T, y_window)
        stacked = lax.psum(jnp.stack(partials + [congruence]), ("row", "col"))
        summed_cross = stacked[:current]
        summed_own = stacked[current]
        y_blocks = []
        for earlier in range(current):
            block_sum = summed_cross[earlier]
            for other_node in range(current):
                block_sum = block_sum + precise(
                    inverse_block(diagonals, crossed, earlier, other_node),
                    factors[pair_index(current, other_node)],
                )
            y_blocks.append(block_sum)
        diagonal = inverses[current] + summed_own
        for earlier in range(current):
            diagonal = diagonal + precise(
                factors[pair_index(current, earlier)].T, y_blocks[earlier]
            )
            crossed[earlier, current] = -y_blocks[earlier]
        columns.append(-y_window)
        diagonals.append(diagonal)
    column_terms = jnp.stack(columns) * pole_weight
    diagonal_terms = (
        jnp.stack(
            [
                lax.dynamic_slice_in_dim(diagonal, row_index * share_rows, share_rows, 0)
                for diagonal in diagonals
            ]
        )
        * pole_weight
    )
    summed_columns, summed_diagonals = (
        lax.psum_scatter(column_terms, "pole", scatter_dimension=1, tiled=True),
        lax.psum_scatter(diagonal_terms, "pole", scatter_dimension=1, tiled=True),
    )
    return (summed_columns[:, None], summed_diagonals)


def solution(mesh):
    return jax.shard_map(
        shards,
        mesh=mesh,
        in_specs=(
            P("pole", "col", "row"),
            P("pole", "col", "row", None),
            P(None, "row"),
            P("pole", None),
            P("pole", None, "row", None),
            P("pole", None, "row", None),
            P(),
            P("pole"),
        ),
        out_specs=(P(None, "col", ("row", "pole"), None), P(None, ("row", "pole"), None)),
        check_vma=False,
    )
```

profile of v0, /device:TPU:0, one launch (start us, length us, event | category | flops | bytes accessed | tf_op | source)
XLA Modules:
  0.0 490.8 jit_solution(11846383781759528025)
XLA Ops:
  7.2 0.7 all-gather.2.cloned.1.call-update
  7.9 1.4 fusion.45
  15.1 0.9 slice_subtract_fusion.1
  16.0 29.3 %all-gather.2.cloned.1.call-done = bf16[1,2,2048,256]{3,2,0,1:T(8,128)(2,1)} async-done(((bf16[1,1,2048,256]{3,2,0,1:T(8,128)(2,1)}), bf16[1,2,2048,256]{3,2,0,1:T(8,128)(2,1)}) %all-gather.2.cloned.1.call-update) | async-done | bytes 2097168 | tf_op jit(solution)/shard_map/all_gather | solution.py:46
  45.4 2.2 dynamic-slice_bitcast_fusion.1
  47.6 9.0 %gather_fusion = bf16[2048,256]{1,0:T(8,128)(2,1)} fusion(bf16[2048,256]{1,0:T(8,128)(2,1)S(1)} %get-tuple-element.12, s32[2048]{0:T(1024)S(1)} %fusion.35), kind=kCustom, calls=%fused_computation.clone | custom fusion | bytes 2105344 | tf_op jit(solution)/shard_map/jit(_take)/gather | solution.py:53
  56.6 1.5 broadcast_select_fusion.2
  58.1 10.5 %fusion.6 = f32[4096,256]{0,1:T(8,128)} fusion(bf16[2048,256]{1,0:T(8,128)(2,1)S(1)} %broadcast_select_fusion.2, bf16[1,4096,2048]{2,1,0:T(8,128)(2,1)} %param.10), kind=kOutput, calls=%fused_computation.9 | convolution fusion | flops 4294967296 | bytes 22020096 | tf_op jit(solution)/shard_map/dot_general | solution.py:26
  68.7 7.5 %gather_fusion.1 = bf16[2048,256]{1,0:T(8,128)(2,1)S(1)} fusion(bf16[2048,256]{1,0:T(8,128)(2,1)S(1)} %get-tuple-element.10, s32[2048]{0:T(1024)S(1)} %fusion.36), kind=kCustom, calls=%fused_computation.1.clone | custom fusion | bytes 2105344 | tf_op jit(solution)/shard_map/jit(_take)/gather | solution.py:53
  76.2 0.4 broadcast_select_fusion.1
  76.7 10.6 %fusion.9 = f32[4096,256]{0,1:T(8,128)} fusion(bf16[2048,256]{1,0:T(8,128)(2,1)S(1)} %broadcast_select_fusion.1, bf16[1,4096,2048]{2,1,0:T(8,128)(2,1)} %param.10), kind=kOutput, calls=%fused_computation.10 | convolution fusion | flops 4294967296 | bytes 22020096 | tf_op jit(solution)/shard_map/dot_general | solution.py:26
  87.4 7.5 %gather_fusion.2 = bf16[2048,256]{1,0:T(8,128)(2,1)S(1)} fusion(bf16[2048,256]{1,0:T(8,128)(2,1)S(1)} %get-tuple-element.11, s32[2048]{0:T(1024)S(1)} %fusion.37), kind=kCustom, calls=%fused_computation.2.clone | custom fusion | bytes 2105344 | tf_op jit(solution)/shard_map/jit(_take)/gather | solution.py:53
  94.9 0.4 broadcast_select_fusion
  95.3 10.6 %fusion.12 = f32[4096,256]{0,1:T(8,128)} fusion(bf16[2048,256]{1,0:T(8,128)(2,1)S(1)} %broadcast_select_fusion, bf16[1,4096,2048]{2,1,0:T(8,128)(2,1)} %param.10), kind=kOutput, calls=%fused_computation.11 | convolution fusion | flops 4294967296 | bytes 22020096 | tf_op jit(solution)/shard_map/dot_general | solution.py:26
  106.0 0.8 copy-done.11
  106.8 20.3 %all_gather.10 = bf16[1,3,256,256]{3,2,1,0:T(8,128)(2,1)S(1)} all-gather(bf16[1,3,64,256]{3,2,1,0:T(8,128)(2,1)S(1)} %copy-done.11), channel_id=1, replica_groups=mesh['row'=4,'col'=2,'pole'=4] {'row'}, dimensions={2}, use_global_device_ids=true | all-gather | bytes 491520 | tf_op jit(solution)/shard_map/all_gather | solution.py:38
  127.2 24.6 %reduce-scatter.6.cloned.1.call-done = f32[1024,256]{0,1:T(8,128)} async-done(((f32[4096,256]{0,1:T(8,128)}), f32[1024,256]{0,1:T(8,128)}) %reduce-scatter.6.cloned.1.call-update) | async-done | bytes 1048592 | tf_op jit(solution)/shard_map/reduce_scatter | solution.py:58
  151.8 79.5 %reduce-scatter.8.cloned.1.call-done = f32[1024,256]{0,1:T(8,128)} async-done(((f32[4096,256]{0,1:T(8,128)}), f32[1024,256]{0,1:T(8,128)}) %reduce-scatter.8.cloned.1.call-update) | async-done | bytes 1048592 | tf_op jit(solution)/shard_map/reduce_scatter | solution.py:58
  231.3 2.2 convolution_add_fusion.2
  233.6 2.5 convolution_bitcast_fusion.6
  236.1 1.3 convolution_bitcast_fusion.4
  237.4 73.4 %reduce-scatter.10.cloned.1.call-done = f32[1024,256]{0,1:T(8,128)} async-done(((f32[4096,256]{0,1:T(8,128)}), f32[1024,256]{0,1:T(8,128)}) %reduce-scatter.10.cloned.1.call-update) | async-done | bytes 1048592 | tf_op jit(solution)/shard_map/reduce_scatter | solution.py:58
  310.8 2.1 convolution_add_fusion.1
  312.9 0.7 convolution_add_fusion
  313.7 0.8 convolution_bitcast_fusion.3
  314.4 0.6 convolution_bitcast_fusion.7
  315.1 0.8 pad_maximum_fusion.1
  315.9 0.6 convolution_bitcast_fusion.5
  316.6 0.9 pad_maximum_fusion
  317.5 1.5 convolution_bitcast_fusion.8
  319.7 0.6 fusion.44
  320.6 2.6 maximum_multiply_fusion
  323.3 31.1 %all_gather.11 = f32[1,3,256,256]{3,2,1,0:T(8,128)S(1)} all-gather(f32[1,3,64,256]{3,2,1,0:T(8,128)S(1)} %copy-done.10), channel_id=1, replica_groups=mesh['row'=4,'col'=2,'pole'=4] {'row'}, dimensions={2}, use_global_device_ids=true | all-gather | bytes 983040 | tf_op jit(solution)/shard_map/all_gather | solution.py:41
  354.4 67.3 %all-reduce.3.cloned.1.call-done = (f32[3,256,256]{2,1,0:T(8,128)}, f32[2,256,256]{2,1,0:T(8,128)}, f32[1,256,256]{2,1,0:T(8,128)}) async-done(((f32[3,256,256]{2,1,0:T(8,128)}, f32[2,256,256]{2,1,0:T(8,128)}, f32[1,256,256]{2,1,0:T(8,128)}), (f32[3,256,256]{2,1,0:T(8,128)}, f32[2,256,256]{2,1,0:T(8,128)}, f32[1,256,256]{2,1,0:T(8,128)})) %all-reduce.3.cloned.1.call-update) | async-done | bytes 1572880 | tf_op jit(solution)/shard_map/psum | solution.py:65
  421.8 0.9 fusion.34
  422.7 1.0 slice_bitcast_fusion.2
  423.6 1.3 convolution_add_fusion.6
  424.9 1.3 convolution_add_fusion.7
  426.3 0.3 convolution_add_fusion.5
  426.5 0.3 convolution_bitcast_fusion.1
  426.9 1.3 convolution_add_fusion.4
  428.2 0.3 fusion.15
  428.5 0.3 convolution_add_fusion.3
  428.8 0.3 convolution_bitcast_fusion
  429.2 1.3 maximum_multiply_fusion.1
  430.5 30.6 %reduce-scatter.12.cloned.1.call-done = f32[3,256,256]{1,2,0:T(8,128)} async-done(((f32[3,1024,256]{1,2,0:T(8,128)}), f32[3,256,256]{1,2,0:T(8,128)}) %reduce-scatter.12.cloned.1.call-update) | async-done | bytes 786448 | tf_op jit(solution)/shard_map/reduce_scatter | solution.py:96
  461.1 2.3 copy.18
  463.4 20.6 %reduce-scatter.14.cloned.1.call-done = f32[3,16,256]{2,1,0:T(8,128)} async-done(((f32[3,64,256]{2,1,0:T(8,128)}), f32[3,16,256]{2,1,0:T(8,128)}) %reduce-scatter.14.cloned.1.call-update) | async-done | bytes 49168 | tf_op jit(solution)/shard_map/reduce_scatter | solution.py:97
  (48 shorter events, 0.8 us)
Async XLA Ops:
  7.2 38.2 %all-gather.2.cloned.1.call-start = ((), (), s32[]{:S(2)}) async-start(), calls=%async_computation.5 | async-start | bytes 3145728 | tf_op jit(solution)/shard_map/all_gather | solution.py:46
  7.9 143.9 %reduce-scatter.6.cloned.1.call-start = ((), (), s32[]{:S(2)}) async-start(), calls=%async_computation.6 | async-start | bytes 5242880 | tf_op jit(solution)/shard_map/reduce_scatter | solution.py:58
  58.1 10.5 %copy-start.5 = (bf16[2048,256]{1,0:T(8,128)(2,1)}, bf16[2048,256]{1,0:T(8,128)(2,1)S(1)}, u32[]{:S(2)}) copy-start(bf16[2048,256]{1,0:T(8,128)(2,1)S(1)} %broadcast_select_fusion.2) | copy-start | bytes 3145732
  68.6 162.7 %reduce-scatter.8.cloned.1.call-start = ((), (), s32[]{:S(2)}) async-start(), calls=%async_computation.7 | async-start | bytes 5242880 | tf_op jit(solution)/shard_map/reduce_scatter | solution.py:58
  76.7 10.6 %copy-start.3 = (bf16[2048,256]{1,0:T(8,128)(2,1)}, bf16[2048,256]{1,0:T(8,128)(2,1)S(1)}, u32[]{:S(2)}) copy-start(bf16[2048,256]{1,0:T(8,128)(2,1)S(1)} %broadcast_select_fusion.1) | copy-start | bytes 3145732
  87.3 223.5 %reduce-scatter.10.cloned.1.call-start = ((), (), s32[]{:S(2)}) async-start(), calls=%async_computation.8 | async-start | bytes 5242880 | tf_op jit(solution)/shard_map/reduce_scatter | solution.py:58
  95.3 140.8 %copy-start.1 = (bf16[2048,256]{1,0:T(8,128)(2,1)}, bf16[2048,256]{1,0:T(8,128)(2,1)S(1)}, u32[]{:S(2)}) copy-start(bf16[2048,256]{1,0:T(8,128)(2,1)S(1)} %broadcast_select_fusion) | copy-start | bytes 3145732
  105.9 0.9 copy-start.11
  105.9 315.8 %all-reduce.3.cloned.1.call-start = ((), (), s32[]{:S(2)}) async-start(), calls=%async_computation.11 | async-start | bytes 3145728 | tf_op jit(solution)/shard_map/psum | solution.py:65
  151.8 159.0 %copy-start = (f32[1024,256]{0,1:T(8,128)S(1)}, f32[1024,256]{0,1:T(8,128)}, u32[]{:S(2)}) copy-start(f32[1024,256]{0,1:T(8,128)} %reduce-scatter.6.cloned.1.call-done) | copy-start | bytes 3145732
  310.8 2.8 copy-start.2
  310.8 3.6 copy-start.4
  312.9 2.2 copy-start.8
  312.9 3.7 copy-start.7
  313.6 3.9 copy-start.6
  315.1 4.6 copy-start.12
  319.0 142.1 %reduce-scatter.12.cloned.1.call-start = ((), (), s32[]{:S(2)}) async-start(), calls=%async_computation.9 | async-start | bytes 3932160 | tf_op jit(solution)/shard_map/reduce_scatter | solution.py:96
  320.6 2.6 copy-start.10
  323.2 160.7 %reduce-scatter.14.cloned.1.call-start = ((), (), s32[]{:S(2)}) async-start(), calls=%async_computation.10 | async-start | bytes 245760 | tf_op jit(solution)/shard_map/reduce_scatter | solution.py:97
  421.8 6.5 %copy-start.9 = (f32[2,256,256]{2,1,0:T(8,128)S(1)}, f32[2,256,256]{2,1,0:T(8,128)}, u32[]{:S(2)}) copy-start(f32[2,256,256]{2,1,0:T(8,128)} %get-tuple-element.8) | copy-start | bytes 1572868
Sparse Core Ops, SparseCore 0:
  9.5 35.8 all-gather.1
  68.8 82.9 reduce-scatter.5
  154.1 77.2 reduce-scatter.7
  233.5 77.2 reduce-scatter.9
  319.2 102.5 all-reduce.2
  424.1 36.9 reduce-scatter.11
  464.1 19.7 reduce-scatter.13
where the time goes:
time: 491 us
  waiting for transfers between devices  326 us (66%)
  blocking collectives  51.5 us (10%)
  matrix products  49.5 us (10%)
  local copies, waits for them, and re-layouts  31.8 us (6%)
  between operations  20.9 us (4%)
  other arithmetic  10.7 us (2%)
    reduce_scatter x3, waiting for transfers between devices, shards(): lax.psum_scatter(window_term(window_block, aligned), 'row', scatter_dimen...  178 us
    psum x1, waiting for transfers between devices, shards(): stacked = lax.psum(jnp.stack(partials + [congruence]), ('row', 'col'))  67.3 us
    dot_general x3, matrix products, window_term(): return jnp.dot(window_block, aligned, preferred_element_type=jnp.float32)  31.7 us
    all_gather x1, blocking collectives, shards(): lax.all_gather(diag_inverse, 'row', axis=2, tiled=True)  31.1 us
    reduce_scatter x1, waiting for transfers between devices, shards(): lax.psum_scatter(column_terms, 'pole', scatter_dimension=1, tiled=True)  30.6 us
    all_gather x1, waiting for transfers between devices, shards(): slot_panels = lax.all_gather(panels, 'col', axis=1, tiled=True)[0]  29.3 us
    gather x3, local copies, waits for them, and re-layouts, shards(): jnp.take(received, row_map[current] - row_index * band_rows, axis=0)  24 us
    reduce_scatter x1, waiting for transfers between devices, shards(): lax.psum_scatter(diagonal_terms, 'pole', scatter_dimension=1, tiled=True)  20.6 us
  transfers between devices with their start and end apart: 7, of which 7 were waited for; matrix products, arithmetic and copies ran while one was open for 12% of the time, Pallas kernels for 0%

commit v1 on v0

--- a/solution.py
+++ b/solution.py
@@ -62,7 +62,7 @@
         for earlier in range(current):
             y_window = y_window + precise(columns[earlier], factors[pair_index(current, earlier)])
         congruence = precise(own_rows.T, y_window)
-        stacked = lax.psum(jnp.stack(partials + [congruence]), ("row", "col"))
+        stacked = lax.psum(lax.psum(jnp.stack(partials + [congruence]), "col"), "row")
         summed_cross = stacked[:current]
         summed_own = stacked[current]
         y_blocks = []

time: 491 us -> 523 us (1.065)
  waiting for transfers between devices: 326 us -> 359 us
    psum x1 -> x2, waiting for transfers between devices: 67.3 us -> 99.8 us  [the longest x1 52.2 us: shards(): lax.psum(jnp.stack(partials + [congruence]), 'col')]
  transfers between devices with their start and end apart: 7 -> 8, of which waited for: 7 -> 8; matrix products, arithmetic and copies ran while one was open for 12% -> 11% of each run, Pallas kernels for 0% -> 0%
where the time goes in v1:
time: 523 us; the launch traced here: 522 us
  waiting for transfers between devices  359 us (69%)
  blocking collectives  50.1 us (10%)
  matrix products  49.6 us (9%)
  local copies, waits for them, and re-layouts  31.8 us (6%)
  between operations  20.9 us (4%)
  other arithmetic  10.9 us (2%)
    reduce_scatter x3, waiting for transfers between devices, shards(): lax.psum_scatter(window_term(window_block, aligned), 'row', scatter_dimen...  178 us
    psum x1, waiting for transfers between devices, shards(): lax.psum(jnp.stack(partials + [congruence]), 'col')  52.2 us
    psum x1, waiting for transfers between devices, shards(): lax.psum(lax.psum(jnp.stack(partials + [congruence]), 'col'), 'row')  47.7 us
    dot_general x3, matrix products, window_term(): return jnp.dot(window_block, aligned, preferred_element_type=jnp.float32)  31.7 us
    reduce_scatter x1, waiting for transfers between devices, shards(): lax.psum_scatter(column_terms, 'pole', scatter_dimension=1, tiled=True)  30.6 us
    all_gather x1, blocking collectives, shards(): lax.all_gather(diag_inverse, 'row', axis=2, tiled=True)  29.8 us
    all_gather x1, waiting for transfers between devices, shards(): slot_panels = lax.all_gather(panels, 'col', axis=1, tiled=True)[0]  29.3 us
    gather x3, local copies, waits for them, and re-layouts, shards(): jnp.take(received, row_map[current] - row_index * band_rows, axis=0)  24 us
  transfers between devices with their start and end apart: 8, of which 8 were waited for; matrix products, arithmetic and copies ran while one was open for 11% of the time, Pallas kernels for 0%

profile of v1, /device:TPU:0, one launch (start us, length us, event | category | flops | bytes accessed | tf_op | source)
XLA Modules:
  0.0 522.2 jit_solution(18153262156397842658)
XLA Ops:
  7.2 0.7 all-gather.2.cloned.1.call-update
  7.9 1.4 fusion.45
  15.1 0.9 slice_subtract_fusion.1
  16.0 29.3 %all-gather.2.cloned.1.call-done = bf16[1,2,2048,256]{3,2,0,1:T(8,128)(2,1)} async-done(((bf16[1,1,2048,256]{3,2,0,1:T(8,128)(2,1)}), bf16[1,2,2048,256]{3,2,0,1:T(8,128)(2,1)}) %all-gather.2.cloned.1.call-update) | async-done | bytes 2097168 | tf_op jit(solution)/shard_map/all_gather | solution.py:46
  45.4 2.3 dynamic-slice_bitcast_fusion.1
  47.6 9.0 %gather_fusion = bf16[2048,256]{1,0:T(8,128)(2,1)} fusion(bf16[2048,256]{1,0:T(8,128)(2,1)S(1)} %get-tuple-element.15, s32[2048]{0:T(1024)S(1)} %fusion.35), kind=kCustom, calls=%fused_computation.clone | custom fusion | bytes 2105344 | tf_op jit(solution)/shard_map/jit(_take)/gather | solution.py:53
  56.6 1.5 broadcast_select_fusion.2
  58.1 10.5 %fusion.6 = f32[4096,256]{0,1:T(8,128)} fusion(bf16[2048,256]{1,0:T(8,128)(2,1)S(1)} %broadcast_select_fusion.2, bf16[1,4096,2048]{2,1,0:T(8,128)(2,1)} %param.10), kind=kOutput, calls=%fused_computation.9 | convolution fusion | flops 4294967296 | bytes 22020096 | tf_op jit(solution)/shard_map/dot_general | solution.py:26
  68.7 7.5 %gather_fusion.1 = bf16[2048,256]{1,0:T(8,128)(2,1)S(1)} fusion(bf16[2048,256]{1,0:T(8,128)(2,1)S(1)} %get-tuple-element.13, s32[2048]{0:T(1024)S(1)} %fusion.36), kind=kCustom, calls=%fused_computation.1.clone | custom fusion | bytes 2105344 | tf_op jit(solution)/shard_map/jit(_take)/gather | solution.py:53
  76.3 0.4 broadcast_select_fusion.1
  76.7 10.6 %fusion.9 = f32[4096,256]{0,1:T(8,128)} fusion(bf16[2048,256]{1,0:T(8,128)(2,1)S(1)} %broadcast_select_fusion.1, bf16[1,4096,2048]{2,1,0:T(8,128)(2,1)} %param.10), kind=kOutput, calls=%fused_computation.10 | convolution fusion | flops 4294967296 | bytes 22020096 | tf_op jit(solution)/shard_map/dot_general | solution.py:26
  87.4 7.5 %gather_fusion.2 = bf16[2048,256]{1,0:T(8,128)(2,1)S(1)} fusion(bf16[2048,256]{1,0:T(8,128)(2,1)S(1)} %get-tuple-element.14, s32[2048]{0:T(1024)S(1)} %fusion.37), kind=kCustom, calls=%fused_computation.2.clone | custom fusion | bytes 2105344 | tf_op jit(solution)/shard_map/jit(_take)/gather | solution.py:53
  94.9 0.4 broadcast_select_fusion
  95.4 10.6 %fusion.12 = f32[4096,256]{0,1:T(8,128)} fusion(bf16[2048,256]{1,0:T(8,128)(2,1)S(1)} %broadcast_select_fusion, bf16[1,4096,2048]{2,1,0:T(8,128)(2,1)} %param.10), kind=kOutput, calls=%fused_computation.11 | convolution fusion | flops 4294967296 | bytes 22020096 | tf_op jit(solution)/shard_map/dot_general | solution.py:26
  106.0 0.8 copy-done.11
  106.8 20.3 %all_gather.10 = bf16[1,3,256,256]{3,2,1,0:T(8,128)(2,1)S(1)} all-gather(bf16[1,3,64,256]{3,2,1,0:T(8,128)(2,1)S(1)} %copy-done.11), channel_id=1, replica_groups=mesh['row'=4,'col'=2,'pole'=4] {'row'}, dimensions={2}, use_global_device_ids=true | all-gather | bytes 491520 | tf_op jit(solution)/shard_map/all_gather | solution.py:38
  127.2 24.6 %reduce-scatter.6.cloned.1.call-done = f32[1024,256]{0,1:T(8,128)} async-done(((f32[4096,256]{0,1:T(8,128)}), f32[1024,256]{0,1:T(8,128)}) %reduce-scatter.6.cloned.1.call-update) | async-done | bytes 1048592 | tf_op jit(solution)/shard_map/reduce_scatter | solution.py:58
  151.8 79.6 %reduce-scatter.8.cloned.1.call-done = f32[1024,256]{0,1:T(8,128)} async-done(((f32[4096,256]{0,1:T(8,128)}), f32[1024,256]{0,1:T(8,128)}) %reduce-scatter.8.cloned.1.call-update) | async-done | bytes 1048592 | tf_op jit(solution)/shard_map/reduce_scatter | solution.py:58
  231.3 2.2 convolution_add_fusion.2
  233.6 2.5 convolution_bitcast_fusion.6
  236.1 1.3 convolution_bitcast_fusion.4
  237.5 73.4 %reduce-scatter.10.cloned.1.call-done = f32[1024,256]{0,1:T(8,128)} async-done(((f32[4096,256]{0,1:T(8,128)}), f32[1024,256]{0,1:T(8,128)}) %reduce-scatter.10.cloned.1.call-update) | async-done | bytes 1048592 | tf_op jit(solution)/shard_map/reduce_scatter | solution.py:58
  310.8 2.1 convolution_add_fusion.1
  312.9 0.7 convolution_add_fusion
  313.7 0.8 convolution_bitcast_fusion.3
  314.5 0.6 convolution_bitcast_fusion.7
  315.1 0.8 pad_maximum_fusion.1
  316.0 0.6 convolution_bitcast_fusion.5
  316.6 0.9 pad_maximum_fusion
  317.6 1.5 convolution_bitcast_fusion.8
  319.1 52.2 %all-reduce.7.cloned.1.call-done = (f32[3,256,256]{2,1,0:T(8,128)}, f32[2,256,256]{2,1,0:T(8,128)}, f32[1,256,256]{2,1,0:T(8,128)}) async-done(((f32[3,256,256]{2,1,0:T(8,128)}, f32[2,256,256]{2,1,0:T(8,128)}, f32[1,256,256]{2,1,0:T(8,128)}), (f32[3,256,256]{2,1,0:T(8,128)}, f32[2,256,256]{2,1,0:T(8,128)}, f32[1,256,256]{2,1,0:T(8,128)})) %all-reduce.7.cloned.1.call-update) | async-done | bytes 1572880 | tf_op jit(solution)/shard_map/psum | solution.py:65
  372.0 0.6 fusion.44
  372.9 2.6 maximum_multiply_fusion
  375.6 29.8 %all_gather.11 = f32[1,3,256,256]{3,2,1,0:T(8,128)S(1)} all-gather(f32[1,3,64,256]{3,2,1,0:T(8,128)S(1)} %copy-done.10), channel_id=1, replica_groups=mesh['row'=4,'col'=2,'pole'=4] {'row'}, dimensions={2}, use_global_device_ids=true | all-gather | bytes 983040 | tf_op jit(solution)/shard_map/all_gather | solution.py:41
  405.5 47.7 %all-reduce.5.cloned.1.call-done = (f32[3,256,256]{2,1,0:T(8,128)}, f32[2,256,256]{2,1,0:T(8,128)}, f32[1,256,256]{2,1,0:T(8,128)}) async-done(((f32[3,256,256]{2,1,0:T(8,128)}, f32[2,256,256]{2,1,0:T(8,128)}, f32[1,256,256]{2,1,0:T(8,128)}), (f32[3,256,256]{2,1,0:T(8,128)}, f32[2,256,256]{2,1,0:T(8,128)}, f32[1,256,256]{2,1,0:T(8,128)})) %all-reduce.5.cloned.1.call-update) | async-done | bytes 1572880 | tf_op jit(solution)/shard_map/psum | solution.py:65
  453.2 0.9 fusion.34
  454.1 1.0 slice_bitcast_fusion.2
  455.0 1.3 convolution_add_fusion.6
  456.4 1.3 convolution_add_fusion.7
  457.9 0.3 convolution_bitcast_fusion.1
  458.3 1.3 convolution_add_fusion.4
  459.6 0.3 fusion.15
  460.0 0.3 convolution_add_fusion.3
  460.2 0.3 convolution_bitcast_fusion
  460.6 1.3 maximum_multiply_fusion.1
  461.9 30.6 %reduce-scatter.12.cloned.1.call-done = f32[3,256,256]{1,2,0:T(8,128)} async-done(((f32[3,1024,256]{1,2,0:T(8,128)}), f32[3,256,256]{1,2,0:T(8,128)}) %reduce-scatter.12.cloned.1.call-update) | async-done | bytes 786448 | tf_op jit(solution)/shard_map/reduce_scatter | solution.py:96
  492.6 2.3 copy.18
  494.8 20.5 %reduce-scatter.14.cloned.1.call-done = f32[3,16,256]{2,1,0:T(8,128)} async-done(((f32[3,64,256]{2,1,0:T(8,128)}), f32[3,16,256]{2,1,0:T(8,128)}) %reduce-scatter.14.cloned.1.call-update) | async-done | bytes 49168 | tf_op jit(solution)/shard_map/reduce_scatter | solution.py:97
  (51 shorter events, 1.2 us)
Async XLA Ops:
  7.2 38.2 %all-gather.2.cloned.1.call-start = ((), (), s32[]{:S(2)}) async-start(), calls=%async_computation.5 | async-start | bytes 3145728 | tf_op jit(solution)/shard_map/all_gather | solution.py:46
  7.9 143.9 %reduce-scatter.6.cloned.1.call-start = ((), (), s32[]{:S(2)}) async-start(), calls=%async_computation.6 | async-start | bytes 5242880 | tf_op jit(solution)/shard_map/reduce_scatter | solution.py:58
  58.1 10.5 %copy-start.5 = (bf16[2048,256]{1,0:T(8,128)(2,1)}, bf16[2048,256]{1,0:T(8,128)(2,1)S(1)}, u32[]{:S(2)}) copy-start(bf16[2048,256]{1,0:T(8,128)(2,1)S(1)} %broadcast_select_fusion.2) | copy-start | bytes 3145732
  68.7 162.7 %reduce-scatter.8.cloned.1.call-start = ((), (), s32[]{:S(2)}) async-start(), calls=%async_computation.7 | async-start | bytes 5242880 | tf_op jit(solution)/shard_map/reduce_scatter | solution.py:58
  76.7 10.6 %copy-start.3 = (bf16[2048,256]{1,0:T(8,128)(2,1)}, bf16[2048,256]{1,0:T(8,128)(2,1)S(1)}, u32[]{:S(2)}) copy-start(bf16[2048,256]{1,0:T(8,128)(2,1)S(1)} %broadcast_select_fusion.1) | copy-start | bytes 3145732
  87.3 223.5 %reduce-scatter.10.cloned.1.call-start = ((), (), s32[]{:S(2)}) async-start(), calls=%async_computation.8 | async-start | bytes 5242880 | tf_op jit(solution)/shard_map/reduce_scatter | solution.py:58
  95.4 140.8 %copy-start.1 = (bf16[2048,256]{1,0:T(8,128)(2,1)}, bf16[2048,256]{1,0:T(8,128)(2,1)S(1)}, u32[]{:S(2)}) copy-start(bf16[2048,256]{1,0:T(8,128)(2,1)S(1)} %broadcast_select_fusion) | copy-start | bytes 3145732
  106.0 0.9 copy-start.11
  106.0 265.3 %all-reduce.7.cloned.1.call-start = ((), (), s32[]{:S(2)}) async-start(), calls=%async_computation.12 | async-start | bytes 3145728 | tf_op jit(solution)/shard_map/psum | solution.py:65
  151.8 159.1 %copy-start = (f32[1024,256]{0,1:T(8,128)S(1)}, f32[1024,256]{0,1:T(8,128)}, u32[]{:S(2)}) copy-start(f32[1024,256]{0,1:T(8,128)} %reduce-scatter.6.cloned.1.call-done) | copy-start | bytes 3145732
  310.8 2.8 copy-start.2
  310.8 3.6 copy-start.4
  312.9 2.2 copy-start.8
  312.9 3.7 copy-start.7
  313.7 3.9 copy-start.6
  316.0 56.0 %copy-start.12 = (f32[4]{0:T(128)S(1)}, f32[4]{0:T(128)}, u32[]{:S(2)}) copy-start(f32[4]{0:T(128)} %param.16) | copy-start | bytes 52
  319.1 134.1 %all-reduce.5.cloned.1.call-start = ((), (), s32[]{:S(2)}) async-start(), calls=%async_computation.11 | async-start | bytes 3145728 | tf_op jit(solution)/shard_map/psum | solution.py:65
  371.3 121.2 %reduce-scatter.12.cloned.1.call-start = ((), (), s32[]{:S(2)}) async-start(), calls=%async_computation.9 | async-start | bytes 3932160 | tf_op jit(solution)/shard_map/reduce_scatter | solution.py:96
  372.9 2.7 copy-start.10
  375.6 139.8 %reduce-scatter.14.cloned.1.call-start = ((), (), s32[]{:S(2)}) async-start(), calls=%async_computation.10 | async-start | bytes 245760 | tf_op jit(solution)/shard_map/reduce_scatter | solution.py:97
  453.2 6.4 %copy-start.9 = (f32[2,256,256]{2,1,0:T(8,128)S(1)}, f32[2,256,256]{2,1,0:T(8,128)}, u32[]{:S(2)}) copy-start(f32[2,256,256]{2,1,0:T(8,128)} %get-tuple-element.8) | copy-start | bytes 1572868
Sparse Core Ops, SparseCore 0:
  9.5 35.8 all-gather.1
  68.8 82.9 reduce-scatter.5
  154.1 77.2 reduce-scatter.7
  233.5 77.2 reduce-scatter.9
  319.2 52.0 all-reduce.6
  373.7 79.4 all-reduce.4
  455.7 36.8 reduce-scatter.11
  495.6 19.7 reduce-scatter.13
